TPU v7x, 512 devices: a whole 4x8x8 slice. The times are simulated.
512 devices in a mesh: section: 4 (over x), seq: 8 (over y), dp: 16 (over z, core).
Axes of the slice: x: 4, y: 8, z: 8, core: 2. Of those that a mesh axis runs over, the one named last changes fastest.
Arguments:
- queries: bfloat16 [16, 1024, 32, 128], P('dp', 'seq', 'section'), may hold values from -18 to 18
- video_keys: bfloat16 [16, 1024, 32, 128], P('dp', 'seq', 'section'), may hold values from -18 to 18
- video_values: bfloat16 [16, 1024, 32, 128], P('dp', 'seq', 'section'), may hold values from -6 to 6
- cross_queries: bfloat16 [16, 1024, 32, 128], P('dp', 'seq', 'section'), may hold values from -8 to 8
- self_cotangent: bfloat16 [16, 1024, 32, 128], P('dp', 'seq', 'section'), may hold values from -6 to 6
- cross_cotangent: bfloat16 [16, 1024, 32, 128], P('dp', 'seq', 'section'), may hold values from -6 to 6
- caption_states: bfloat16 [16, 512, 4096], P('dp', 'seq'), may hold values from -400 to 400
- caption_gain: float32 [4096], replicated, may hold values from 0.25 to 1.75
- key_weight: bfloat16 [4096, 4096], P('dp', ('section', 'seq')), may hold values from -0.09375 to 0.09375
- value_weight: bfloat16 [4096, 4096], P('dp', ('section', 'seq')), may hold values from -0.09375 to 0.09375
- video_length: int32 [16], replicated, may hold values from 512 to 1024, as said below
- caption_length: int32 [16], replicated, may hold values from 128 to 512, as said below
Outputs:
- query_gradient: bfloat16 [16, 1024, 32, 128], P('dp', 'seq', 'section')
- key_gradient: bfloat16 [16, 1024, 32, 128], P('dp', 'seq', 'section')
- value_gradient: bfloat16 [16, 1024, 32, 128], P('dp', 'seq', 'section')
- cross_query_gradient: bfloat16 [16, 1024, 32, 128], P('dp', 'seq', 'section')
- key_weight_gradient: float32 [4096, 4096], P('dp', ('section', 'seq'))
- value_weight_gradient: float32 [4096, 4096], P('dp', ('section', 'seq'))
Inputs may be any that keep to these rules, and one draw needn't show every extreme that they name: `video_length`: some clip has all 1024 tokens valid. `caption_length`: some clip has all 512 caption tokens valid.
All inputs are finite; a program needn't handle non-finite values.
Results may differ from a plain program's by a relative error of at most 0.018.
Values may be sent and summed in bfloat16 or wider, within the bound.
A program may use at most 64 MiB of HBM per device.

v0:
```python
import math

import jax
import jax.numpy as jnp
from jax import lax
from jax.sharding import PartitionSpec as P

norm_epsilon = 1e-06


def sent_together(arrays, axis, dim, along):
    ends, at = ([], 0)
    for a in arrays[:-1]:
        at += a.shape[along]
        ends.append(at)
    both = jnp.concatenate(arrays, axis=along)
    return tuple(jnp.split(lax.all_gather(both, axis, axis=dim, tiled=True), ends, axis=along))


def side_by_side(arrays, axis, split_dim, concat_dim, along):
    widths = [a.shape[along] for a in arrays]
    both = jnp.concatenate(arrays, axis=along)
    out = lax.all_to_all(both, axis, split_axis=split_dim, concat_axis=concat_dim, tiled=True)
    return tuple(jnp.split(out, [sum(widths[:k]) for k in range(1, len(widths))], axis=along))


def normalize_rows(states, caption_gain):
    values = states.astype(jnp.float32)
    mean_square = jnp.mean(values * values, axis=-1, keepdims=True)
    return (values * lax.rsqrt(mean_square + norm_epsilon) * caption_gain).astype(jnp.bfloat16)


def block_gradients(query_rows, cotangent_rows, key_rows, value_rows, key_limit, score_scale):
    scores = (
        jnp.einsum("qhd,khd->hqk", query_rows, key_rows, preferred_element_type=jnp.float32)
        * score_scale
    )
    columns = lax.broadcasted_iota(jnp.int32, scores.shape, 2)
    scores = jnp.where(columns < key_limit, scores, -jnp.inf)
    maxima = jnp.max(scores, axis=-1, keepdims=True)
    powers = jnp.exp(scores - maxima)
    weights = powers / jnp.sum(powers, axis=-1, keepdims=True)
    weights_low = weights.astype(jnp.bfloat16)
    weight_grad = jnp.einsum(
        "qhd,khd->hqk", cotangent_rows, value_rows, preferred_element_type=jnp.float32
    )
    row_total = jnp.sum(weights * weight_grad, axis=-1, keepdims=True)
    score_grad = (weights * (weight_grad - row_total) * score_scale).astype(jnp.bfloat16)
    query_grad = jnp.einsum(
        "hqk,khd->qhd", score_grad, key_rows, preferred_element_type=jnp.float32
    )
    key_grad = jnp.einsum(
        "hqk,qhd->khd", score_grad, query_rows, preferred_element_type=jnp.float32
    )
    value_grad = jnp.einsum(
        "hqk,qhd->khd", weights_low, cotangent_rows, preferred_element_type=jnp.float32
    )
    return (query_grad, key_grad, value_grad)


def attention_gradients(query_set, cotangent_set, key_set, value_set, key_limit, score_scale):
    row_count = query_set.shape[0]
    block_rows = math.gcd(row_count, 512)
    block_count = row_count // block_rows
    query_blocks = query_set.reshape((block_count, block_rows) + query_set.shape[1:])
    cotangent_blocks = cotangent_set.reshape((block_count, block_rows) + cotangent_set.shape[1:])

    def advance(totals, inputs):
        query_grad, key_grad, value_grad = block_gradients(
            inputs[0], inputs[1], key_set, value_set, key_limit, score_scale
        )
        return ((totals[0] + key_grad, totals[1] + value_grad), query_grad)

    empty = jnp.zeros(key_set.shape, jnp.float32)
    totals, query_grads = lax.scan(advance, (empty, empty), (query_blocks, cotangent_blocks))
    return (query_grads.reshape(query_set.shape), totals[0], totals[1])


def local(
    queries,
    video_keys,
    video_values,
    cross_queries,
    self_cotangent,
    cross_cotangent,
    caption_states,
    caption_gain,
    key_weight,
    value_weight,
    video_length,
    caption_length,
):
    head_size = queries.shape[3]
    score_scale = 1.0 / math.sqrt(head_size)
    head_width = key_weight.shape[1]
    local_heads = head_width // head_size
    normed = normalize_rows(lax.all_gather(caption_states, "seq", axis=1, tiled=True), caption_gain)
    normed_text = normed[0]
    caption_rows = normed_text.shape[0]
    pieces = sent_together((key_weight, value_weight), "dp", 0, 1)
    columns = normed_text
    text_keys = jnp.dot(columns, pieces[0], preferred_element_type=jnp.float32)
    text_values = jnp.dot(columns, pieces[1], preferred_element_type=jnp.float32)
    text_keys = text_keys.astype(jnp.bfloat16).reshape(caption_rows, local_heads, head_size)
    text_values = text_values.astype(jnp.bfloat16).reshape(caption_rows, local_heads, head_size)
    gathered = side_by_side(
        (queries, video_keys, video_values, cross_queries, self_cotangent, cross_cotangent),
        "seq",
        2,
        1,
        0,
    )
    head_queries, head_keys, head_values, head_cross, self_rows, cross_rows = (
        tensor[0] for tensor in gathered
    )
    clip_index = lax.axis_index("dp")
    video_limit = lax.dynamic_index_in_dim(video_length, clip_index, 0, keepdims=False)
    caption_limit = lax.dynamic_index_in_dim(caption_length, clip_index, 0, keepdims=False)
    positions = lax.broadcasted_iota(jnp.int32, (head_queries.shape[0], 1, 1), 0)
    nothing = jnp.zeros((), jnp.bfloat16)
    self_rows = jnp.where(positions < video_limit, self_rows, nothing)
    cross_rows = jnp.where(positions < video_limit, cross_rows, nothing)
    query_grad, key_grad, value_grad = attention_gradients(
        head_queries, self_rows, head_keys, head_values, video_limit, score_scale
    )
    cross_grad, text_key_grad, text_value_grad = attention_gradients(
        head_cross, cross_rows, text_keys, text_values, caption_limit, score_scale
    )
    returned = side_by_side(
        (
            query_grad.astype(jnp.bfloat16)[None],
            key_grad.astype(jnp.bfloat16)[None],
            value_grad.astype(jnp.bfloat16)[None],
            cross_grad.astype(jnp.bfloat16)[None],
        ),
        "seq",
        1,
        2,
        0,
    )
    key_cot = text_key_grad.astype(jnp.bfloat16).reshape(caption_rows, head_width)
    value_cot = text_value_grad.astype(jnp.bfloat16).reshape(caption_rows, head_width)
    stacked = jnp.concatenate((key_cot, value_cot), axis=1)
    contract_rows = (((0,), (0,)), ((), ()))
    columns = normed_text
    gradients = lax.psum_scatter(
        lax.dot_general(columns, stacked, contract_rows, preferred_element_type=jnp.float32).astype(
            jnp.bfloat16
        ),
        "dp",
        scatter_dimension=0,
        tiled=True,
    ).astype(jnp.float32)
    return (
        returned[0],
        returned[1],
        returned[2],
        returned[3],
        gradients[:, :head_width],
        gradients[:, head_width:],
    )


def solution(mesh):
    placed = (
        P("dp", "seq", "section", None),
        P("dp", "seq", "section", None),
        P("dp", "seq", "section", None),
        P("dp", "seq", "section", None),
        P("dp", "seq", "section", None),
        P("dp", "seq", "section", None),
        P("dp", "seq", None),
        P(),
        P("dp", ("section", "seq")),
        P("dp", ("section", "seq")),
        P(),
        P(),
    )
    return jax.shard_map(
        local,
        mesh=mesh,
        in_specs=placed,
        out_specs=(
            P("dp", "seq", "section", None),
            P("dp", "seq", "section", None),
            P("dp", "seq", "section", None),
            P("dp", "seq", "section", None),
            P("dp", ("section", "seq")),
            P("dp", ("section", "seq")),
        ),
        check_vma=False,
    )
```

profile of v0, /device:TPU:1, one launch (start us, length us, event | category | flops | bytes accessed | tf_op | source)
XLA Modules:
  0.0 237.0 jit_solution(1283080764883097908)
XLA Ops:
  8.0 1.5 pad_maximum_fusion.1
  9.6 1.7 copy_dynamic-update-slice_fusion.5
  11.3 1.7 copy_dynamic-update-slice_fusion.4
  13.8 0.8 copy_dynamic-update-slice_fusion.2
  14.5 0.8 copy_dynamic-update-slice_fusion.1
  16.1 7.6 %all-to-all-start = ((bf16[6,128,8,128]{3,1,0,2:T(8,128)(2,1)}), bf16[6,128,8,128]{3,1,0,2:T(8,128)(2,1)S(1)}, u32[]{:S(2)}, u32[]{:S(2)}) async-start(bf16[6,128,8,128]{3,1,0,2:T(8,128)(2,1)} %copy_dynamic-update-slice_fusion), calls=%async_computation | async-start | bytes 3145728 | tf_op jit(solution)/shard_map/all_to_all | solution.py:23
  25.7 53.7 %all-to-all-done = bf16[6,128,8,128]{3,1,0,2:T(8,128)(2,1)S(1)} async-done(((bf16[6,128,8,128]{3,1,0,2:T(8,128)(2,1)}), bf16[6,128,8,128]{3,1,0,2:T(8,128)(2,1)S(1)}, u32[]{:S(2)}, u32[]{:S(2)}) %all-to-all-start) | async-done | bytes 1572896 | tf_op jit(solution)/shard_map/all_to_all | solution.py:23
  79.5 0.8 fusion.65
  80.4 0.9 select_bitcast_fusion.1
  81.3 20.1 %all-gather.3.cloned.1.call-done = bf16[1,512,4096]{2,1,0:T(8,128)(2,1)} async-done(((bf16[1,64,4096]{2,1,0:T(8,128)(2,1)}), bf16[1,512,4096]{2,1,0:T(8,128)(2,1)}) %all-gather.3.cloned.1.call-update) | async-done | bytes 4194320 | tf_op jit(solution)/shard_map/all_gather | solution.py:97
  101.4 3.1 %fusion.49 = f32[512]{0:T(512)S(1)} fusion(bf16[1,512,4096]{2,1,0:T(8,128)(2,1)} %all-gather.3.cloned.1.call-done), kind=kLoop, calls=%fused_computation.65 | loop fusion | flops 6290944 | bytes 4196352 | tf_op jit(solution)/shard_map/reduce_sum | solution.py:29
  104.5 44.8 %all-gather.5.cloned.1.call-done = bf16[4096,256]{1,0:T(8,128)(2,1)} async-done(((bf16[256,256]{1,0:T(8,128)(2,1)}), bf16[4096,256]{1,0:T(8,128)(2,1)}) %all-gather.5.cloned.1.call-update) | async-done | bytes 2097168 | tf_op jit(solution)/shard_map/all_gather | solution.py:17
  149.3 3.9 %fusion.53 = bf16[512,1,128]{2,0,1:T(8,128)(2,1)S(1)} fusion(bf16[4096,256]{1,0:T(8,128)(2,1)} %all-gather.5.cloned.1.call-done, bf16[1,512,4096]{2,1,0:T(8,128)(2,1)} %all-gather.3.cloned.1.call-done, f32[4096]{0:T(1024)S(1)} %copy-done.9, f32[512]{0:T(512)S(1)} %add_rsqrt_fusion), kind=kOutput, calls=%fused_computation.73 | convolution fusion | flops 545325056 | bytes 5392384 | tf_op jit(solution)/shard_map/dot_general | solution.py:102
  153.7 1.3 fusion.54
  155.1 8.4 %while.31 = (s32[]{:T(128)}, f32[512,1,128]{0,2,1:T(8,128)}, f32[512,1,128]{0,2,1:T(8,128)S(1)}, bf16[2,512,1,128]{3,1,2,0:T(8,128)(2,1)S(1)}, bf16[2,512,1,128]...) while((s32[]{:T(128)}, f32[512,1,128]{0,2,1:T(8,128)}, ...), condition=%wide.region_10.11_spmd.clone, body=%wide.region_6.10_spmd.clone.sunk | while | flops 340524032 | bytes 11164816 | solution.py:75
  157.5 1.0 fusion.112
  161.1 2.0 fusion.112
  163.5 1.1 convert_bitcast_fusion.2
  164.6 5.2 %convolution_convert_fusion = bf16[4096,256]{1,0:T(8,128)(2,1)} fusion(bf16[512,128]{0,1:T(8,128)(2,1)S(1)} %get-tuple-element.309, bf16[512,128]{0,1:T(8,128)(2,1)S(1)} %get-tuple-element.310, bf16[1,512,4096]{2,1,0:T(8,128)(2,1)} %all-gather.3.cloned.1.call-done, f32[4096]{0:T(1024)S(1)} %copy-done.9, f32[512]{0:T(512)S(1)} %add_rsqrt_fusion), kind=kOutput, calls=%fused_computation.68 | convolution fusion | flops 1083703296 | bytes 6572032 | tf_op jit(solution)/shard_map/dot_general | solution.py:147
  169.9 13.7 %while.30 = (s32[]{:T(128)}, f32[1024,1,128]{0,2,1:T(8,128)S(1)}, f32[1024,1,128]{0,2,1:T(8,128)}, bf16[2,512,1,128]{3,1,2,0:T(8,128)(2,1)S(1)}, bf16[2,512,1,12...) while((s32[]{:T(128)}, f32[1024,1,128]{0,2,1:T(8,128)S(1)}, ...), condition=%wide.region_4.5_spmd.clone, body=%wide.region_0.4_spmd.clone.sunk | while | flops 685243904 | bytes 23622340 | solution.py:75
  171.7 2.6 %fusion.102 = f32[1024,1,128]{0,2,1:T(8,128)} fusion(f32[1024,1,128]{0,2,1:T(8,128)} %get-tuple-element.483, pred[]{:T(512)S(6)} %compare.6, bf16[2,512,1,128]{3,1,2,0:T(8,128)(2,1)} %get-tuple-element.499, s32[]{:T(128)} %get-tuple-element.481, f32[512,1024]{1,0:T(8,128)S(1)} %get-tuple-element.420, f32[512]{0:T(512)S(1)} %fusion.100, ...), kind=kOutput, calls=%fused_computation.10.clone.1 | convolution fusion | flops 137101312 | bytes 3282433 | tf_op jit(solution)/shard_map/while/body/eval_jaxpr/hqk,qhd->khd/dot_general | solution.py:55
  178.4 2.8 %fusion.102 = f32[1024,1,128]{0,2,1:T(8,128)} fusion(f32[1024,1,128]{0,2,1:T(8,128)} %get-tuple-element.483, pred[]{:T(512)S(6)} %compare.6, bf16[2,512,1,128]{3,1,2,0:T(8,128)(2,1)} %get-tuple-element.499, s32[]{:T(128)} %get-tuple-element.481, f32[512,1024]{1,0:T(8,128)S(1)} %get-tuple-element.420, f32[512]{0:T(512)S(1)} %fusion.100, ...), kind=kOutput, calls=%fused_computation.10.clone.1 | convolution fusion | flops 137101312 | bytes 3282433 | tf_op jit(solution)/shard_map/while/body/eval_jaxpr/hqk,qhd->khd/dot_general | solution.py:55
  183.6 1.2 copy.73
  185.0 1.1 pad_maximum_fusion
  186.1 0.8 copy.77
  186.9 34.8 %all_to_all.30 = bf16[4,1024,1,128]{3,0,2,1:T(4,128)(2,1)S(1)} all-to-all(bf16[4,1024,1,128]{3,0,2,1:T(4,128)(2,1)S(1)} %copy.77), channel_id=1, replica_groups=mesh['section'=4,'seq'=8,'dp'=16] {'seq'}, dimensions={1} | all-to-all | bytes 2097152 | tf_op jit(solution)/shard_map/all_to_all | solution.py:23
  222.0 0.9 copy.79
  222.8 0.9 copy.80
  223.7 0.9 copy.81
  224.6 0.9 copy.82
  225.5 3.4 %reduce-scatter.2.cloned.1.call-done = bf16[256,256]{1,0:T(8,128)(2,1)} async-done(((bf16[4096,256]{1,0:T(8,128)(2,1)}), bf16[256,256]{1,0:T(8,128)(2,1)}) %reduce-scatter.2.cloned.1.call-update) | async-done | bytes 131088 | tf_op jit(solution)/shard_map/reduce_scatter | solution.py:146
  228.9 1.6 fusion.66
  (78 shorter events, 18.7 us)
Async XLA Ops:
  7.2 5.8 %copy-start.3 = (bf16[1,128,8,128]{3,2,1,0:T(8,128)(2,1)S(1)}, bf16[1,128,8,128]{3,2,1,0:T(8,128)(2,1)}, u32[]{:S(2)}) copy-start(bf16[1,128,8,128]{3,2,1,0:T(8,128)(2,1)} %param.18) | copy-start | bytes 786436
  7.2 6.6 %copy-start.4 = (bf16[1,128,8,128]{3,2,1,0:T(8,128)(2,1)S(1)}, bf16[1,128,8,128]{3,2,1,0:T(8,128)(2,1)}, u32[]{:S(2)}) copy-start(bf16[1,128,8,128]{3,2,1,0:T(8,128)(2,1)} %param.19) | copy-start | bytes 786436
  7.2 7.3 %copy-start.5 = (bf16[1,128,8,128]{3,2,1,0:T(8,128)(2,1)S(1)}, bf16[1,128,8,128]{3,2,1,0:T(8,128)(2,1)}, u32[]{:S(2)}) copy-start(bf16[1,128,8,128]{3,2,1,0:T(8,128)(2,1)} %param.20) | copy-start | bytes 786436
  7.2 8.1 %copy-start.6 = (bf16[1,128,8,128]{3,2,1,0:T(8,128)(2,1)S(1)}, bf16[1,128,8,128]{3,2,1,0:T(8,128)(2,1)}, u32[]{:S(2)}) copy-start(bf16[1,128,8,128]{3,2,1,0:T(8,128)(2,1)} %param.21) | copy-start | bytes 786436
  7.2 94.2 %all-gather.3.cloned.1.call-start = ((), (), s32[]{:S(2)}) async-start(), calls=%async_computation.3 | async-start | bytes 4718592 | tf_op jit(solution)/shard_map/all_gather | solution.py:97
  7.9 141.3 %all-gather.5.cloned.1.call-start = ((), (), s32[]{:S(2)}) async-start(), calls=%async_computation.4 | async-start | bytes 2228224 | tf_op jit(solution)/shard_map/all_gather | solution.py:17
  14.5 9.3 %copy-start.10 = (s32[16]{0:T(128)S(1)}, s32[16]{0:T(128)}, u32[]{:S(2)}) copy-start(s32[16]{0:T(128)} %param.26) | copy-start | bytes 196
  14.5 9.9 %copy-start.11 = (s32[16]{0:T(128)S(1)}, s32[16]{0:T(128)}, u32[]{:S(2)}) copy-start(s32[16]{0:T(128)} %param.27) | copy-start | bytes 196
  16.1 63.3 %all-to-all-start = ((bf16[6,128,8,128]{3,1,0,2:T(8,128)(2,1)}), bf16[6,128,8,128]{3,1,0,2:T(8,128)(2,1)S(1)}, u32[]{:S(2)}, u32[]{:S(2)}) async-start(bf16[6,128,8,128]{3,1,0,2:T(8,128)(2,1)} %copy_dynamic-update-slice_fusion), calls=%async_computation | async-start | bytes 3145728 | tf_op jit(solution)/shard_map/all_to_all | solution.py:23
  23.7 205.2 %reduce-scatter.2.cloned.1.call-start = ((), (), s32[]{:S(2)}) async-start(), calls=%async_computation.5 | async-start | bytes 2228224 | tf_op jit(solution)/shard_map/reduce_scatter | solution.py:146
  81.3 68.0 %copy-start.9 = (f32[4096]{0:T(1024)S(1)}, f32[4096]{0:T(1024)}, u32[]{:S(2)}) copy-start(f32[4096]{0:T(1024)} %param.23) | copy-start | bytes 49156
  149.3 4.0 %copy-start = (bf16[1,512,4096]{2,1,0:T(8,128)(2,1)S(1)}, bf16[1,512,4096]{2,1,0:T(8,128)(2,1)}, u32[]{:S(2)}) copy-start(bf16[1,512,4096]{2,1,0:T(8,128)(2,1)} %all-gather.3.cloned.1.call-done) | copy-start | bytes 12582916
  149.3 4.4 %copy-start.8 = (bf16[4096,256]{1,0:T(8,128)(2,1)S(1)}, bf16[4096,256]{1,0:T(8,128)(2,1)}, u32[]{:S(2)}) copy-start(bf16[4096,256]{1,0:T(8,128)(2,1)} %all-gather.5.cloned.1.call-done) | copy-start | bytes 6291460
  163.5 6.3 %copy-start.1 = (bf16[2,512,1,128]{3,1,2,0:T(8,128)(2,1)}, bf16[2,512,1,128]{3,1,2,0:T(8,128)(2,1)S(1)}, u32[]{:S(2)}) copy-start(bf16[2,512,1,128]{3,1,2,0:T(8,128)(2,1)S(1)} %get-tuple-element.107) | copy-start | bytes 786436
  171.7 2.6 %copy-start.2 = (bf16[1024,1,128]{2,0,1:T(8,128)(2,1)S(1)}, bf16[1024,1,128]{2,0,1:T(8,128)(2,1)}, u32[]{:S(2)}) copy-start(bf16[1024,1,128]{2,0,1:T(8,128)(2,1)} %get-tuple-element.500) | copy-start | bytes 786436 | tf_op jit(solution)/shard_map/while
  171.7 2.6 %copy-start.7 = (bf16[2,512,1,128]{3,1,2,0:T(8,128)(2,1)S(1)}, bf16[2,512,1,128]{3,1,2,0:T(8,128)(2,1)}, u32[]{:S(2)}) copy-start(bf16[2,512,1,128]{3,1,2,0:T(8,128)(2,1)} %get-tuple-element.499) | copy-start | bytes 786436 | tf_op jit(solution)/shard_map/while
  178.4 2.8 %copy-start.2 = (bf16[1024,1,128]{2,0,1:T(8,128)(2,1)S(1)}, bf16[1024,1,128]{2,0,1:T(8,128)(2,1)}, u32[]{:S(2)}) copy-start(bf16[1024,1,128]{2,0,1:T(8,128)(2,1)} %get-tuple-element.500) | copy-start | bytes 786436 | tf_op jit(solution)/shard_map/while
  178.4 2.8 %copy-start.7 = (bf16[2,512,1,128]{3,1,2,0:T(8,128)(2,1)S(1)}, bf16[2,512,1,128]{3,1,2,0:T(8,128)(2,1)}, u32[]{:S(2)}) copy-start(bf16[2,512,1,128]{3,1,2,0:T(8,128)(2,1)} %get-tuple-element.499) | copy-start | bytes 786436 | tf_op jit(solution)/shard_map/while
Sparse Core Ops, SparseCore 0:
  10.1 91.2 all-gather.2
  104.1 45.1 all-gather.4
  170.0 58.8 reduce-scatter.1
where the time goes:
time: 240 us; the launch traced here: 237 us
  waiting for transfers between devices  123 us (51%)
  blocking collectives  34.8 us (14%)
  matrix products  26 us (11%)
  local copies, waits for them, and re-layouts  16.8 us (7%)
  other arithmetic  14.5 us (6%)
  between operations  13.9 us (6%)
  starting transfers between devices  7.75 us (3%)
    all_to_all x1, waiting for transfers between devices, side_by_side(): lax.all_to_all(both, axis, split_axis=split_dim, concat_axis=concat_dim,...  53.7 us
    all_gather x1, waiting for transfers between devices, sent_together(): lax.all_gather(both, axis, axis=dim, tiled=True)  44.8 us
    all_to_all x1, blocking collectives, side_by_side(): lax.all_to_all(both, axis, split_axis=split_dim, concat_axis=concat_dim,...  34.8 us
    all_gather x1, waiting for transfers between devices, local(): lax.all_gather(caption_states, 'seq', axis=1, tiled=True)  20.1 us
    unnamed x29, local copies, waits for them, and re-layouts  9.76 us
    all_to_all x1, starting transfers between devices, side_by_side(): lax.all_to_all(both, axis, split_axis=split_dim, concat_axis=concat_dim,...  7.64 us
    dot_general x4, matrix products, block_gradients(): jnp.einsum('hqk,qhd->khd', weights_low, cotangent_rows, preferred_element...  6.09 us
    dot_general x1, matrix products, local(): lax.dot_general(columns, stacked, contract_rows, preferred_element_type=j...  5.25 us
  transfers between devices with their start and end apart: 4, of which 4 were waited for; matrix products, arithmetic and copies ran while one was open for 15% of the time, Pallas kernels for 0%

commit v1 on v0

v1 whole, which is shorter than its diff:
```python
import functools
import math

import jax
import jax.numpy as jnp
from jax import lax
from jax.experimental import pallas as pl
from jax.experimental.pallas import tpu as pltpu
from jax.sharding import PartitionSpec as P

norm_epsilon = 1e-06
f32, bf16 = jnp.float32, jnp.bfloat16
mesh_ids = pl.DeviceIdType.MESH


def far_first(n):
    return sorted(range(1, n), key=lambda k: (-min(k, n - k), k))


def dot(a, b, contract):
    return lax.dot_general(a, b, ((contract[:1], contract[1:]), ((), ())), preferred_element_type=f32)


def kernel(
    sizes,
    blocks, caption, gain, weight, limits,
    video_out, weight_out,
    inbuf, capbuf, normed, wbuf, text, key_turned, key_total, value_total, grads,
    cot_turned, mine, pair_out, pair_in, ring_out, ring_in,
    send, recv, here,
):
    nx, ny, nz = sizes
    tokens, size = inbuf.shape[1:]
    part = tokens // ny
    cap_rows, width = caption.shape
    captions = cap_rows * ny
    quarter = width // nx
    wrows = weight.shape[0]
    s, q, d = lax.axis_index("section"), lax.axis_index("seq"), lax.axis_index("dp")
    z, c = d // 2, lax.rem(d, 2)
    partner = {"dp": 2 * z + 1 - c}
    scale = 1.0 / math.sqrt(size)
    video_limit, caption_limit = limits[0], limits[1]

    def at_x(k):
        return {"section": lax.rem(s + k, nx)}

    def at_y(k):
        return {"seq": lax.rem(q + k, ny)}

    def at_z(k):
        return {"dp": 2 * lax.rem(z + k, nz) + c}

    barrier = pltpu.get_barrier_semaphore()
    peers = [at_x(k) for k in range(1, nx)] + [at_y(k) for k in range(1, ny)]
    peers += [at_z(k) for k in range(1, nz)] + [partner]
    for peer in peers:
        pl.semaphore_signal(barrier, inc=1, device_id=peer, device_id_type=mesh_ids)
    pl.semaphore_wait(barrier, len(peers))

    used = [0]
    every = []

    def push(src, dst, peer):
        n = used[0]
        used[0] += 1
        copy = pltpu.make_async_remote_copy(
            src_ref=src, dst_ref=dst, send_sem=send.at[n], recv_sem=recv.at[n],
            device_id=peer, device_id_type=mesh_ids,
        )
        copy.start()
        every.append(copy)
        return copy

    def rows(index, count):
        return pl.ds(pl.multiple_of(index * count, count), count)

    my_quarter = rows(s, quarter)
    ys, zs = far_first(ny), far_first(nz)

    cap_y = {
        k: push(caption.at[:, my_quarter], capbuf.at[q, :, my_quarter], at_y(k)) for k in ys
    }
    w_z = {k: push(weight, wbuf.at[rows(d, wrows)], at_z(k)) for k in zs}
    w_pair = [push(weight, wbuf.at[rows(d, wrows)], partner)]
    self_y, cross_y = {}, {}
    for k in ys:
        to = lax.rem(q + k, ny)
        self_y[k] = push(
            blocks.at[to, pl.ds(0, 4)], inbuf.at[pl.ds(0, 4), rows(q, part)], at_y(k)
        )
    for k in ys:
        to = lax.rem(q + k, ny)
        cross_y[k] = push(
            blocks.at[to, pl.ds(4, 2)], inbuf.at[pl.ds(4, 2), rows(q, part)], at_y(k)
        )
    own = [
        pltpu.make_async_copy(blocks.at[q], inbuf.at[:, rows(q, part)], here.at[0]),
        pltpu.make_async_copy(caption, capbuf.at[q], here.at[1]),
        pltpu.make_async_copy(weight, wbuf.at[rows(d, wrows)], here.at[2]),
    ]
    for copy in own:
        copy.start()

    cap_x = []
    for k in reversed(ys):
        cap_y[k].wait_recv()
        piece = capbuf.at[lax.rem(q + ny - k, ny), :, my_quarter]
        for j in far_first(nx):
            cap_x.append(push(piece, piece, at_x(j)))
    for k in reversed(zs):
        w_z[k].wait_recv()
        piece = wbuf.at[rows(2 * lax.rem(z + nz - k, nz) + c, wrows)]
        w_pair.append(push(piece, piece, partner))
    for copy in own:
        copy.wait()

    def attend(key, value, query_ref, cot_ref, limit, keys, query_out):
        block = math.gcd(tokens, 256)
        key_turned[:, :keys] = key[...].astype(f32).T.astype(bf16)
        key_total[pl.ds(0, keys)] = jnp.zeros((keys, size), f32)
        value_total[pl.ds(0, keys)] = jnp.zeros((keys, size), f32)

        def step(i, carry):
            span = rows(i, block)
            query = query_ref[span, :]
            at = lax.broadcasted_iota(jnp.int32, (block, size), 0) + i * block
            cot = jnp.where(at < video_limit, cot_ref[span, :].astype(f32), 0.0).astype(bf16)
            scores = dot(key[...], query, (1, 1)) * (scale * math.log2(math.e))
            key_at = lax.broadcasted_iota(jnp.int32, (keys, block), 0)
            scores = jnp.where(key_at < limit, scores, -jnp.inf)
            powers = jnp.exp2(scores - jnp.max(scores, axis=0, keepdims=True))
            inverse = 1.0 / jnp.sum(powers, axis=0, keepdims=True)
            weights = powers * inverse
            weight_grad = dot(value[...], cot, (1, 1))
            total = jnp.sum(weights * weight_grad, axis=0, keepdims=True)
            score_grad = (weights * (weight_grad - total) * scale).astype(bf16)
            value_total[pl.ds(0, keys)] += dot(weights.astype(bf16), cot, (1, 0))
            key_total[pl.ds(0, keys)] += dot(score_grad, query, (1, 0))
            query_out[span, :] = dot(key_turned[:, :keys], score_grad, (1, 0)).T.astype(bf16)
            return carry

        lax.fori_loop(0, tokens // block, step, 0)

    for k in ys:
        self_y[k].wait_recv()
    attend(inbuf.at[1], inbuf.at[2], inbuf.at[0], inbuf.at[3], video_limit, tokens, grads.at[0])
    grads[1] = key_total[...].astype(bf16)
    grads[2] = value_total[...].astype(bf16)
    back = []
    for k in ys:
        to = lax.rem(q + k, ny)
        back.append(
            push(grads.at[pl.ds(0, 3), rows(to, part)], video_out.at[pl.ds(0, 3), q], at_y(k))
        )

    for copy in cap_x + w_pair:
        copy.wait_recv()

    def normalize(i, carry):
        values = capbuf[i].astype(f32)
        mean = jnp.mean(values * values, axis=-1, keepdims=True)
        normed[rows(i, cap_rows), :] = (
            values * lax.rsqrt(mean + norm_epsilon) * gain[...]
        ).astype(bf16)
        return carry

    lax.fori_loop(0, ny, normalize, 0)
    text_block = math.gcd(captions, 256)

    def project(i, carry):
        span = rows(i, text_block)
        text[span, :] = dot(normed[span, :], wbuf[...], (1, 0)).astype(bf16)
        return carry

    lax.fori_loop(0, captions // text_block, project, 0)

    for k in ys:
        cross_y[k].wait_recv()
    attend(
        text.at[:, pl.ds(0, size)], text.at[:, pl.ds(size, size)], inbuf.at[4], inbuf.at[5],
        caption_limit, captions, grads.at[3],
    )
    for k in ys:
        to = lax.rem(q + k, ny)
        back.append(push(grads.at[3, rows(to, part)], video_out.at[3, q], at_y(k)))
    cot_turned[pl.ds(0, size), :] = key_total[pl.ds(0, captions)].T.astype(bf16)
    cot_turned[pl.ds(size, size), :] = value_total[pl.ds(0, captions)].T.astype(bf16)

    order = zs + [0]
    pair, ring = [], []

    def finish(i):
        pair[i].wait_recv()
        total = mine[i] + pair_in[i].astype(f32)
        if i < nz - 1:
            ring_out[i] = total.astype(bf16)
            ring.append(push(ring_out.at[i], ring_in.at[i], at_z(order[i])))
        else:
            mine[i] = total

    for i, k in enumerate(order):
        to = 2 * lax.rem(z + k, nz)
        theirs = dot(cot_turned[...], normed[:, rows(to + 1 - c, wrows)], (1, 0))
        pair_out[i] = theirs.astype(bf16)
        pair.append(push(pair_out.at[i], pair_in.at[i], partner))
        mine[i] = dot(cot_turned[...], normed[:, rows(to + c, wrows)], (1, 0))
        if i:
            finish(i - 1)
    finish(nz - 1)
    keep = pltpu.make_async_copy(grads.at[:, rows(q, part)], video_out.at[:, q], here.at[3])
    keep.start()
    total = mine[nz - 1]
    for i, copy in enumerate(ring):
        copy.wait_recv()
        total += ring_in[i].astype(f32)
    weight_out[...] = total.T
    keep.wait()
    for copy in back:
        copy.wait_recv()
    for copy in every:
        copy.wait_send()


def local(
    sizes,
    queries, video_keys, video_values, cross_queries, self_cotangent, cross_cotangent,
    caption_states, caption_gain, key_weight, value_weight, video_length, caption_length,
):
    nx, ny, nz = sizes
    part, heads, size = queries.shape[1:]
    tokens = part * ny
    cap_rows, width = caption_states.shape[1:]
    captions = cap_rows * ny
    wrows = key_weight.shape[0]
    blocks = jnp.concatenate(
        (queries, video_keys, video_values, self_cotangent, cross_queries, cross_cotangent)
    ).transpose(2, 0, 1, 3)
    clip = lax.axis_index("dp")
    limits = jnp.stack([
        lax.dynamic_index_in_dim(video_length, clip, 0, keepdims=False),
        lax.dynamic_index_in_dim(caption_length, clip, 0, keepdims=False),
    ])
    weight = jnp.concatenate((key_weight, value_weight), axis=1)
    copies = (ny - 1) * (1 + (nx - 1) + 2 + 2) + (nz - 1) + nz + nz + (nz - 1)
    vmem = pl.BlockSpec(memory_space=pltpu.VMEM)
    video, weights = pl.pallas_call(
        functools.partial(kernel, sizes),
        out_shape=(
            jax.ShapeDtypeStruct((4, ny, part, size), bf16),
            jax.ShapeDtypeStruct((wrows, 2 * size), f32),
        ),
        in_specs=[vmem] * 4 + [pl.BlockSpec(memory_space=pltpu.SMEM)],
        out_specs=(vmem, vmem),
        scratch_shapes=[
            pltpu.VMEM((6, tokens, size), bf16),
            pltpu.VMEM((ny, cap_rows, width), bf16),
            pltpu.VMEM((captions, width), bf16),
            pltpu.VMEM((width, 2 * size), bf16),
            pltpu.VMEM((captions, 2 * size), bf16),
            pltpu.VMEM((size, max(tokens, captions)), bf16),
            pltpu.VMEM((max(tokens, captions), size), f32),
            pltpu.VMEM((max(tokens, captions), size), f32),
            pltpu.VMEM((4, tokens, size), bf16),
            pltpu.VMEM((2 * size, captions), bf16),
            pltpu.VMEM((nz, 2 * size, wrows), f32),
            pltpu.VMEM((nz, 2 * size, wrows), bf16),
            pltpu.VMEM((nz, 2 * size, wrows), bf16),
            pltpu.VMEM((nz - 1, 2 * size, wrows), bf16),
            pltpu.VMEM((nz - 1, 2 * size, wrows), bf16),
            pltpu.SemaphoreType.DMA((copies,)),
            pltpu.SemaphoreType.DMA((copies,)),
            pltpu.SemaphoreType.DMA((4,)),
        ],
        compiler_params=pltpu.CompilerParams(
            collective_id=0, has_side_effects=True, vmem_limit_bytes=60 * 1024 * 1024
        ),
    )(blocks, caption_states[0], caption_gain[None], weight, limits)
    video = video.transpose(0, 2, 1, 3)
    return (
        video[0:1], video[1:2], video[2:3], video[3:4],
        weights[:, :size], weights[:, size:],
    )


def solution(mesh):
    token = P("dp", "seq", "section", None)
    weight = P("dp", ("section", "seq"))
    sizes = (mesh.shape["section"], mesh.shape["seq"], mesh.shape["dp"] // 2)
    return jax.shard_map(
        functools.partial(local, sizes),
        mesh=mesh,
        in_specs=(token,) * 6 + (P("dp", "seq", None), P(), weight, weight, P(), P()),
        out_specs=(token,) * 4 + (weight, weight),
        check_vma=False,
    )
```

time: 240 us -> 134 us (0.56); the launches traced: 237 us -> 134 us
  waiting for transfers between devices: 123 us -> 0 us
  Pallas kernels: 0 us -> 120 us
  blocking collectives: 34.8 us -> 0 us
  matrix products: 26 us -> 0 us
  between operations: 13.9 us -> 0.79 us
  other arithmetic: 14.5 us -> 2.61 us
  starting transfers between devices: 7.75 us -> 0 us
  local copies, waits for them, and re-layouts: 16.8 us -> 10 us
    pallas_call x0 -> x1, Pallas kernels: none -> 120 us  [local(): pl.pallas_call(functools.partial(kernel, sizes), out_shape=(jax.ShapeDtyp...]
    all_gather x2 -> x0, waiting for transfers between devices: 64.9 us -> none  [the longest x1 44.8 us: sent_together(): lax.all_gather(both, axis, axis=dim, tiled=True)]
    all_to_all x1 -> x0, waiting for transfers between devices: 53.7 us -> none  [side_by_side(): lax.all_to_all(both, axis, split_axis=split_dim, concat_axis=concat_dim,...]
    all_to_all x1 -> x0, blocking collectives: 34.8 us -> none  [side_by_side(): lax.all_to_all(both, axis, split_axis=split_dim, concat_axis=concat_dim,...]
    dot_general x23 -> x0, matrix products: 26 us -> none  [the longest x4 6.09 us: block_gradients(): jnp.einsum('hqk,qhd->khd', weights_low, cotangent_rows, preferred_element...]
    all_to_all x1 -> x0, starting transfers between devices: 7.64 us -> none  [side_by_side(): lax.all_to_all(both, axis, split_axis=split_dim, concat_axis=concat_dim,...]
    reduce_sum x5 -> x0, other arithmetic: 4.62 us -> none  [the longest x1 3.08 us: normalize_rows(): mean_square = jnp.mean(values * values, axis=-1, keepdims=True)]
    reduce_scatter x1 -> x0, waiting for transfers between devices: 3.43 us -> none  [local(): lax.psum_scatter(lax.dot_general(columns, stacked, contract_rows, preferr...]
  transfers between devices with their start and end apart: 4 -> 0, of which waited for: 4 -> 0; matrix products, arithmetic and copies ran while one was open for 15% -> 0% of each run, Pallas kernels for 0% -> 0%
where the time goes in v1:
time: 134 us
  Pallas kernels  120 us (90%)
  local copies, waits for them, and re-layouts  10 us (7%)
  other arithmetic  2.61 us (2%)
    pallas_call x1, Pallas kernels, local(): pl.pallas_call(functools.partial(kernel, sizes), out_shape=(jax.ShapeDtyp...  120 us
    unnamed x27, local copies, waits for them, and re-layouts  6.77 us

profile of v1, /device:TPU:1, one launch (start us, length us, event | category | flops | bytes accessed | tf_op | source)
XLA Modules:
  0.0 133.7 jit_solution(2676185594767464899)
XLA Ops:
  0.6 0.0 copy-start.1
  0.6 0.0 copy-start.2
  0.7 0.0 copy-start.3
  0.7 0.0 copy-start.5
  0.7 0.0 copy-start.6
  0.7 1.1 copy_dynamic-update-slice_fusion.5
  1.7 0.0 copy-start.7
  1.8 0.0 copy-start.8
  1.8 1.0 copy_dynamic-update-slice_fusion.4
  2.8 1.0 copy_dynamic-update-slice_fusion.3
  3.8 0.0 copy-done.1
  3.8 0.1 copy_dynamic-update-slice_fusion.2
  3.9 0.0 copy-done.2
  3.9 0.1 copy_dynamic-update-slice_fusion.1
  4.0 0.0 copy-done.3
  4.0 0.1 copy_dynamic-update-slice_fusion
  4.0 0.0 copy-start
  4.1 0.0 copy-done.5
  4.1 0.0 copy-done.6
  4.1 0.7 pad_maximum_fusion.weight
  4.8 0.6 dynamic_slice.8
  5.4 0.6 dynamic_slice.7
  6.0 1.9 %pad_add_fusion.limits = s32[2]{0:T(128)} fusion(s32[1]{0:T(128)} %dynamic_slice.8, s32[1]{0:T(128)} %dynamic_slice.7), kind=kLoop, calls=%fused_computation.7 | loop fusion | flops 2 | bytes 16 | tf_op jit(solution)/shard_map/stack | solution.py:240
  7.9 0.0 copy-done
  7.9 120.3 %shard_map.163 = (bf16[4,8,128,128]{3,2,1,0:T(8,128)(2,1)}, f32[256,256]{1,0:T(8,128)}) custom-call(bf16[8,6,128,128]{3,2,1,0:T(8,128)(2,1)} %bitcast.4, bf16[64,4096]{1,0:T(8,128)(2,1)} %bitcast.6, f32[1,4096]{1,0:T(1,128)} %bitcast.7, bf16[256,256]{1,0:T(8,128)(2,1)} %pad_maximum_fusion.weight, s32[2]{0:T(128)} %pad_add_fusion.limits), custom_call_target="tpu_custom_call" | custom-call | tf_op jit(solution)/shard_map/pallas_call | solution.py:247
  128.1 1.3 fusion
  129.4 0.0 copy-start.4
  129.5 0.9 copy.24
  130.3 0.9 copy.25
  131.2 0.9 copy.26
  132.1 0.9 copy.27
  133.0 0.7 fusion.1
  (3 shorter events, 0.0 us)
Async XLA Ops:
  0.6 3.2 %copy-start.1 = (bf16[1,128,8,128]{3,2,1,0:T(8,128)(2,1)S(1)}, bf16[1,128,8,128]{3,2,1,0:T(8,128)(2,1)}, u32[]{:S(2)}) copy-start(bf16[1,128,8,128]{3,2,1,0:T(8,128)(2,1)} %param.16) | copy-start | bytes 786436
  0.6 3.3 %copy-start.2 = (bf16[1,128,8,128]{3,2,1,0:T(8,128)(2,1)S(1)}, bf16[1,128,8,128]{3,2,1,0:T(8,128)(2,1)}, u32[]{:S(2)}) copy-start(bf16[1,128,8,128]{3,2,1,0:T(8,128)(2,1)} %param.15) | copy-start | bytes 786436
  0.7 3.3 %copy-start.3 = (bf16[1,128,8,128]{3,2,1,0:T(8,128)(2,1)S(1)}, bf16[1,128,8,128]{3,2,1,0:T(8,128)(2,1)}, u32[]{:S(2)}) copy-start(bf16[1,128,8,128]{3,2,1,0:T(8,128)(2,1)} %param.17) | copy-start | bytes 786436
  0.7 3.4 %copy-start.5 = (bf16[256,128]{1,0:T(8,128)(2,1)S(1)}, bf16[256,128]{1,0:T(8,128)(2,1)}, u32[]{:S(2)}) copy-start(bf16[256,128]{1,0:T(8,128)(2,1)} %param.21) | copy-start | bytes 196612
  0.7 3.4 %copy-start.6 = (bf16[256,128]{1,0:T(8,128)(2,1)S(1)}, bf16[256,128]{1,0:T(8,128)(2,1)}, u32[]{:S(2)}) copy-start(bf16[256,128]{1,0:T(8,128)(2,1)} %param.20) | copy-start | bytes 196612
  1.7 3.1 %copy-start.7 = (s32[16]{0:T(128)S(1)}, s32[16]{0:T(128)}, u32[]{:S(2)}) copy-start(s32[16]{0:T(128)} %param.23) | copy-start | bytes 196
  1.8 3.6 %copy-start.8 = (s32[16]{0:T(128)S(1)}, s32[16]{0:T(128)}, u32[]{:S(2)}) copy-start(s32[16]{0:T(128)} %param.22) | copy-start | bytes 196
  4.0 3.8 %copy-start = (bf16[6,128,8,128]{3,1,0,2:T(8,128)(2,1)}, bf16[6,128,8,128]{3,1,0,2:T(8,128)(2,1)S(1)}, u32[]{:S(2)}) copy-start(bf16[6,128,8,128]{3,1,0,2:T(8,128)(2,1)S(1)} %copy_dynamic-update-slice_fusion) | copy-start | bytes 4718596
  129.4 3.5 %copy-start.4 = (f32[256,256]{1,0:T(8,128)S(1)}, f32[256,256]{1,0:T(8,128)}, u32[]{:S(2)}) copy-start(f32[256,256]{1,0:T(8,128)} %get-tuple-element.9) | copy-start | bytes 786436

commit v2 on v1

--- a/solution.py
+++ b/solution.py
@@ -23,8 +23,8 @@
 
 def kernel(
     sizes,
-    blocks, caption, gain, weight, limits,
-    video_out, weight_out,
+    blocks, caption, gain, key_weight, value_weight, video_length, caption_length,
+    query_out, key_out, value_out, cross_out, key_weight_out, value_weight_out,
     inbuf, capbuf, normed, wbuf, text, key_turned, key_total, value_total, grads,
     cot_turned, mine, pair_out, pair_in, ring_out, ring_in,
     send, recv, here,
@@ -35,12 +35,12 @@
     cap_rows, width = caption.shape
     captions = cap_rows * ny
     quarter = width // nx
-    wrows = weight.shape[0]
+    wrows = key_weight.shape[0]
     s, q, d = lax.axis_index("section"), lax.axis_index("seq"), lax.axis_index("dp")
     z, c = d // 2, lax.rem(d, 2)
     partner = {"dp": 2 * z + 1 - c}
     scale = 1.0 / math.sqrt(size)
-    video_limit, caption_limit = limits[0], limits[1]
+    video_limit, caption_limit = video_length[d], caption_length[d]
 
     def at_x(k):
         return {"section": lax.rem(s + k, nx)}
@@ -81,39 +81,75 @@
     cap_y = {
         k: push(caption.at[:, my_quarter], capbuf.at[q, :, my_quarter], at_y(k)) for k in ys
     }
-    w_z = {k: push(weight, wbuf.at[rows(d, wrows)], at_z(k)) for k in zs}
-    w_pair = [push(weight, wbuf.at[rows(d, wrows)], partner)]
+    mine_w = wbuf.at[rows(d, wrows)]
+    own = [
+        pltpu.make_async_copy(key_weight, mine_w.at[:, pl.ds(0, size)], here.at[0]),
+        pltpu.make_async_copy(value_weight, mine_w.at[:, pl.ds(size, size)], here.at[1]),
+        pltpu.make_async_copy(blocks.at[q], inbuf.at[:, rows(q, part)], here.at[2]),
+        pltpu.make_async_copy(caption, capbuf.at[q], here.at[3]),
+    ]
+    for copy in own:
+        copy.start()
     self_y, cross_y = {}, {}
+    for k in ys:
+        to = lax.rem(q + k, ny)
+        cross_y[k] = push(
+            blocks.at[to, pl.ds(4, 2)], inbuf.at[pl.ds(4, 2), rows(q, part)], at_y(k)
+        )
     for k in ys:
         to = lax.rem(q + k, ny)
         self_y[k] = push(
             blocks.at[to, pl.ds(0, 4)], inbuf.at[pl.ds(0, 4), rows(q, part)], at_y(k)
         )
-    for k in ys:
-        to = lax.rem(q + k, ny)
-        cross_y[k] = push(
-            blocks.at[to, pl.ds(4, 2)], inbuf.at[pl.ds(4, 2), rows(q, part)], at_y(k)
-        )
-    own = [
-        pltpu.make_async_copy(blocks.at[q], inbuf.at[:, rows(q, part)], here.at[0]),
-        pltpu.make_async_copy(caption, capbuf.at[q], here.at[1]),
-        pltpu.make_async_copy(weight, wbuf.at[rows(d, wrows)], here.at[2]),
-    ]
-    for copy in own:
-        copy.start()
-
-    cap_x = []
+    own[0].wait()
+    own[1].wait()
+    w_z = {k: push(mine_w, mine_w, at_z(k)) for k in zs}
+    w_pair = [push(mine_w, mine_w, partner)]
+
+    near = {}
     for k in reversed(ys):
         cap_y[k].wait_recv()
         piece = capbuf.at[lax.rem(q + ny - k, ny), :, my_quarter]
-        for j in far_first(nx):
-            cap_x.append(push(piece, piece, at_x(j)))
+        near[k] = [push(piece, piece, at_x(j)) for j in sorted({1, nx - 1})]
+    passed = {k: [] for k in ys}
+    for k in reversed(ys):
+        for copy in near[k]:
+            copy.wait_recv()
+        if nx == 4:
+            half = cap_rows // 2
+            for j, at in ((1, 0), (3, half)):
+                from_quarter = rows(lax.rem(s + nx - j, nx), quarter)
+                piece = capbuf.at[lax.rem(q + ny - k, ny), pl.ds(at, half), from_quarter]
+                passed[k].append(push(piece, piece, at_x(j)))
     for k in reversed(zs):
         w_z[k].wait_recv()
         piece = wbuf.at[rows(2 * lax.rem(z + nz - k, nz) + c, wrows)]
         w_pair.append(push(piece, piece, partner))
-    for copy in own:
-        copy.wait()
+    own[2].wait()
+    own[3].wait()
+
+    def normalize(i):
+        values = capbuf[i].astype(f32)
+        mean = jnp.mean(values * values, axis=-1, keepdims=True)
+        normed[rows(i, cap_rows), :] = (
+            values * lax.rsqrt(mean + norm_epsilon) * gain[...]
+        ).astype(bf16)
+
+    normalize(q)
+    for k in reversed(ys):
+        for copy in passed[k]:
+            copy.wait_recv()
+        normalize(lax.rem(q + ny - k, ny))
+    for copy in w_pair:
+        copy.wait_recv()
+    text_block = math.gcd(captions, 256)
+
+    def project(i, carry):
+        span = rows(i, text_block)
+        text[span, :] = dot(normed[span, :], wbuf[...], (1, 0)).astype(bf16)
+        return carry
+
+    lax.fori_loop(0, captions // text_block, project, 0)
 
     def attend(key, value, query_ref, cot_ref, limit, keys, query_out):
         block = math.gcd(tokens, 256)
@@ -142,38 +178,15 @@
 
         lax.fori_loop(0, tokens // block, step, 0)
 
-    for k in ys:
-        self_y[k].wait_recv()
-    attend(inbuf.at[1], inbuf.at[2], inbuf.at[0], inbuf.at[3], video_limit, tokens, grads.at[0])
-    grads[1] = key_total[...].astype(bf16)
-    grads[2] = value_total[...].astype(bf16)
-    back = []
-    for k in ys:
-        to = lax.rem(q + k, ny)
-        back.append(
-            push(grads.at[pl.ds(0, 3), rows(to, part)], video_out.at[pl.ds(0, 3), q], at_y(k))
-        )
-
-    for copy in cap_x + w_pair:
-        copy.wait_recv()
-
-    def normalize(i, carry):
-        values = capbuf[i].astype(f32)
-        mean = jnp.mean(values * values, axis=-1, keepdims=True)
-        normed[rows(i, cap_rows), :] = (
-            values * lax.rsqrt(mean + norm_epsilon) * gain[...]
-        ).astype(bf16)
-        return carry
-
-    lax.fori_loop(0, ny, normalize, 0)
-    text_block = math.gcd(captions, 256)
-
-    def project(i, carry):
-        span = rows(i, text_block)
-        text[span, :] = dot(normed[span, :], wbuf[...], (1, 0)).astype(bf16)
-        return carry
-
-    lax.fori_loop(0, captions // text_block, project, 0)
+    back, kept = [], []
+
+    def give(i, out):
+        for k in ys:
+            to = lax.rem(q + k, ny)
+            back.append(push(grads.at[i, rows(to, part)], out.at[q], at_y(k)))
+        copy = pltpu.make_async_copy(grads.at[i, rows(q, part)], out.at[q], here.at[4 + i])
+        copy.start()
+        kept.append(copy)
 
     for k in ys:
         cross_y[k].wait_recv()
@@ -181,9 +194,7 @@
         text.at[:, pl.ds(0, size)], text.at[:, pl.ds(size, size)], inbuf.at[4], inbuf.at[5],
         caption_limit, captions, grads.at[3],
     )
-    for k in ys:
-        to = lax.rem(q + k, ny)
-        back.append(push(grads.at[3, rows(to, part)], video_out.at[3, q], at_y(k)))
+    give(3, cross_out)
     cot_turned[pl.ds(0, size), :] = key_total[pl.ds(0, captions)].T.astype(bf16)
     cot_turned[pl.ds(size, size), :] = value_total[pl.ds(0, captions)].T.astype(bf16)
 
@@ -208,14 +219,23 @@
         if i:
             finish(i - 1)
     finish(nz - 1)
-    keep = pltpu.make_async_copy(grads.at[:, rows(q, part)], video_out.at[:, q], here.at[3])
-    keep.start()
+    for k in ys:
+        self_y[k].wait_recv()
+    attend(inbuf.at[1], inbuf.at[2], inbuf.at[0], inbuf.at[3], video_limit, tokens, grads.at[0])
+    give(0, query_out)
+    grads[1] = key_total[...].astype(bf16)
+    give(1, key_out)
+    grads[2] = value_total[...].astype(bf16)
+    give(2, value_out)
     total = mine[nz - 1]
     for i, copy in enumerate(ring):
         copy.wait_recv()
         total += ring_in[i].astype(f32)
-    weight_out[...] = total.T
-    keep.wait()
+    turned = total.T
+    key_weight_out[...] = turned[:, :size]
+    value_weight_out[...] = turned[:, size:]
+    for copy in kept:
+        copy.wait()
     for copy in back:
         copy.wait_recv()
     for copy in every:
@@ -236,22 +256,17 @@
     blocks = jnp.concatenate(
         (queries, video_keys, video_values, self_cotangent, cross_queries, cross_cotangent)
     ).transpose(2, 0, 1, 3)
-    clip = lax.axis_index("dp")
-    limits = jnp.stack([
-        lax.dynamic_index_in_dim(video_length, clip, 0, keepdims=False),
-        lax.dynamic_index_in_dim(caption_length, clip, 0, keepdims=False),
-    ])
-    weight = jnp.concatenate((key_weight, value_weight), axis=1)
-    copies = (ny - 1) * (1 + (nx - 1) + 2 + 2) + (nz - 1) + nz + nz + (nz - 1)
+    copies = (ny - 1) * (1 + 4 + 2 + 4) + (nz - 1) + nz + nz + (nz - 1)
     vmem = pl.BlockSpec(memory_space=pltpu.VMEM)
-    video, weights = pl.pallas_call(
+    smem = pl.BlockSpec(memory_space=pltpu.SMEM)
+    *video, key_grad, value_grad = pl.pallas_call(
         functools.partial(kernel, sizes),
         out_shape=(
-            jax.ShapeDtypeStruct((4, ny, part, size), bf16),
-            jax.ShapeDtypeStruct((wrows, 2 * size), f32),
+            (jax.ShapeDtypeStruct((ny, part, size), bf16),) * 4
+            + (jax.ShapeDtypeStruct((wrows, size), f32),) * 2
         ),
-        in_specs=[vmem] * 4 + [pl.BlockSpec(memory_space=pltpu.SMEM)],
-        out_specs=(vmem, vmem),
+        in_specs=[vmem] * 5 + [smem] * 2,
+        out_specs=(vmem,) * 6,
         scratch_shapes=[
             pltpu.VMEM((6, tokens, size), bf16),
             pltpu.VMEM((ny, cap_rows, width), bf16),
@@ -270,17 +285,16 @@
             pltpu.VMEM((nz - 1, 2 * size, wrows), bf16),
             pltpu.SemaphoreType.DMA((copies,)),
             pltpu.SemaphoreType.DMA((copies,)),
-            pltpu.SemaphoreType.DMA((4,)),
+            pltpu.SemaphoreType.DMA((8,)),
         ],
         compiler_params=pltpu.CompilerParams(
             collective_id=0, has_side_effects=True, vmem_limit_bytes=60 * 1024 * 1024
         ),
-    )(blocks, caption_states[0], caption_gain[None], weight, limits)
-    video = video.transpose(0, 2, 1, 3)
-    return (
-        video[0:1], video[1:2], video[2:3], video[3:4],
-        weights[:, :size], weights[:, size:],
+    )(
+        blocks, caption_states[0], caption_gain[None], key_weight, value_weight,
+        video_length, caption_length,
     )
+    return tuple(a.transpose(1, 0, 2)[None] for a in video) + (key_grad, value_grad)
 
 
 def solution(mesh):

time: 134 us -> 125 us (0.933)
  Pallas kernels: 120 us -> 112 us
  other arithmetic: 2.61 us -> 0 us
  local copies, waits for them, and re-layouts: 10 us -> 12.2 us
    pallas_call x1, Pallas kernels: 120 us -> 112 us  [local(): pl.pallas_call(functools.partial(kernel, sizes), out_shape=(jax.ShapeDtyp...]
    unnamed x27 -> x25, local copies, waits for them, and re-layouts: 6.77 us -> 12.1 us
    slice x2 -> x0, local copies, waits for them, and re-layouts: 2.01 us -> none  [the longest x1 1.29 us: local(): video[3:4]]
    another operation x1 -> x0, other arithmetic: 1.88 us -> none  [local(): jnp.stack([lax.dynamic_index_in_dim(video_length, clip, 0, keepdims=False...]
where the time goes in v2:
time: 125 us
  Pallas kernels  112 us (90%)
  local copies, waits for them, and re-layouts  12.2 us (10%)
    pallas_call x1, Pallas kernels, local(): pl.pallas_call(functools.partial(kernel, sizes), out_shape=(jax.ShapeDtyp...  112 us
    unnamed x25, local copies, waits for them, and re-layouts  12.1 us

profile of v2, /device:TPU:1, one launch (start us, length us, event | category | flops | bytes accessed | tf_op | source)
XLA Modules:
  0.0 124.7 jit_solution(16552474943536715114)
XLA Ops:
  0.6 0.0 copy-start.3
  0.6 0.0 copy-start.1
  0.7 0.0 copy-start.2
  0.7 1.1 copy_dynamic-update-slice_fusion.5
  1.7 1.0 copy_dynamic-update-slice_fusion.4
  2.7 1.0 copy_dynamic-update-slice_fusion.3
  3.8 0.0 copy-done.1
  3.8 0.1 copy_dynamic-update-slice_fusion.2
  3.8 0.0 copy-done.2
  3.8 0.1 copy_dynamic-update-slice_fusion.1
  3.9 0.0 copy-done.3
  3.9 0.1 copy_dynamic-update-slice_fusion
  4.0 0.0 copy-start
  4.0 1.1 copy-done
  5.1 111.8 %shard_map.163 = (bf16[8,128,128]{2,1,0:T(8,128)(2,1)}, bf16[8,128,128]{2,1,0:T(8,128)(2,1)}, bf16[8,128,128]{2,1,0:T(8,128)(2,1)}, bf16[8,128,128]{2,1,0:T(8,12...) custom-call(bf16[8,6,128,128]{3,2,1,0:T(8,128)(2,1)} %bitcast.15, bf16[64,4096]{1,0:T(8,128)(2,1)} %bitcast.16, ...), custom_call_target="tpu_custom_call" | custom-call | tf_op jit(solution)/shard_map/pallas_call | solution.py:262
  117.0 0.0 copy-start.4
  117.0 0.0 copy-start.6
  117.0 0.0 copy-start.5
  117.0 1.9 %copy.24 = bf16[1,128,8,128]{3,2,1,0:T(8,128)(2,1)} copy(bf16[1,128,8,128]{3,1,2,0:T(8,128)(2,1)} %bitcast.20) | data formatting | bytes 524288
  118.9 1.8 %copy.25 = bf16[1,128,8,128]{3,2,1,0:T(8,128)(2,1)} copy(bf16[1,128,8,128]{3,1,2,0:T(8,128)(2,1)} %bitcast.19) | data formatting | bytes 524288
  120.7 1.8 %copy.26 = bf16[1,128,8,128]{3,2,1,0:T(8,128)(2,1)} copy(bf16[1,128,8,128]{3,1,2,0:T(8,128)(2,1)} %bitcast.18) | data formatting | bytes 524288
  122.5 0.0 copy-done.4
  122.5 0.9 copy.27
  123.4 0.0 copy-done.6
  123.4 0.7 copy.41
  124.1 0.0 copy-done.5
  124.1 0.7 copy.42
Async XLA Ops:
  0.6 3.3 %copy-start.3 = (bf16[1,128,8,128]{3,2,1,0:T(8,128)(2,1)S(1)}, bf16[1,128,8,128]{3,2,1,0:T(8,128)(2,1)}, u32[]{:S(2)}) copy-start(bf16[1,128,8,128]{3,2,1,0:T(8,128)(2,1)} %param.17) | copy-start | bytes 786436
  0.6 3.1 %copy-start.1 = (bf16[1,128,8,128]{3,2,1,0:T(8,128)(2,1)S(1)}, bf16[1,128,8,128]{3,2,1,0:T(8,128)(2,1)}, u32[]{:S(2)}) copy-start(bf16[1,128,8,128]{3,2,1,0:T(8,128)(2,1)} %param.16) | copy-start | bytes 786436
  0.7 3.2 %copy-start.2 = (bf16[1,128,8,128]{3,2,1,0:T(8,128)(2,1)S(1)}, bf16[1,128,8,128]{3,2,1,0:T(8,128)(2,1)}, u32[]{:S(2)}) copy-start(bf16[1,128,8,128]{3,2,1,0:T(8,128)(2,1)} %param.15) | copy-start | bytes 786436
  4.0 1.1 copy-start
  117.0 5.6 %copy-start.4 = (bf16[8,128,128]{2,1,0:T(8,128)(2,1)S(1)}, bf16[8,128,128]{2,1,0:T(8,128)(2,1)}, u32[]{:S(2)}) copy-start(bf16[8,128,128]{2,1,0:T(8,128)(2,1)} %get-tuple-element.15) | copy-start | bytes 786436
  117.0 6.4 %copy-start.6 = (f32[256,128]{1,0:T(8,128)S(1)}, f32[256,128]{1,0:T(8,128)}, u32[]{:S(2)}) copy-start(f32[256,128]{1,0:T(8,128)} %get-tuple-element.34) | copy-start | bytes 393220
  117.0 7.1 %copy-start.5 = (f32[256,128]{1,0:T(8,128)S(1)}, f32[256,128]{1,0:T(8,128)}, u32[]{:S(2)}) copy-start(f32[256,128]{1,0:T(8,128)} %get-tuple-element.35) | copy-start | bytes 393220

commit v3 on v2

--- a/solution.py
+++ b/solution.py
@@ -34,7 +34,8 @@
     part = tokens // ny
     cap_rows, width = caption.shape
     captions = cap_rows * ny
-    quarter = width // nx
+    direct = width // 4
+    quarter = (width - direct) // nx
     wrows = key_weight.shape[0]
     s, q, d = lax.axis_index("section"), lax.axis_index("seq"), lax.axis_index("dp")
     z, c = d // 2, lax.rem(d, 2)
@@ -75,12 +76,16 @@
     def rows(index, count):
         return pl.ds(pl.multiple_of(index * count, count), count)
 
-    my_quarter = rows(s, quarter)
+    def features(index):
+        return pl.ds(pl.multiple_of(direct + index * quarter, 128), quarter)
+
+    my_quarter, shared = features(s), pl.ds(0, direct)
     ys, zs = far_first(ny), far_first(nz)
 
     cap_y = {
         k: push(caption.at[:, my_quarter], capbuf.at[q, :, my_quarter], at_y(k)) for k in ys
     }
+    cap_d = {k: push(caption.at[:, shared], capbuf.at[q, :, shared], at_y(k)) for k in ys}
     mine_w = wbuf.at[rows(d, wrows)]
     own = [
         pltpu.make_async_copy(key_weight, mine_w.at[:, pl.ds(0, size)], here.at[0]),
@@ -118,7 +123,7 @@
         if nx == 4:
             half = cap_rows // 2
             for j, at in ((1, 0), (3, half)):
-                from_quarter = rows(lax.rem(s + nx - j, nx), quarter)
+                from_quarter = features(lax.rem(s + nx - j, nx))
                 piece = capbuf.at[lax.rem(q + ny - k, ny), pl.ds(at, half), from_quarter]
                 passed[k].append(push(piece, piece, at_x(j)))
     for k in reversed(zs):
@@ -137,7 +142,7 @@
 
     normalize(q)
     for k in reversed(ys):
-        for copy in passed[k]:
+        for copy in passed[k] + [cap_d[k]]:
             copy.wait_recv()
         normalize(lax.rem(q + ny - k, ny))
     for copy in w_pair:
@@ -256,7 +261,7 @@
     blocks = jnp.concatenate(
         (queries, video_keys, video_values, self_cotangent, cross_queries, cross_cotangent)
     ).transpose(2, 0, 1, 3)
-    copies = (ny - 1) * (1 + 4 + 2 + 4) + (nz - 1) + nz + nz + (nz - 1)
+    copies = (ny - 1) * (1 + 1 + 4 + 2 + 4) + (nz - 1) + nz + nz + (nz - 1)
     vmem = pl.BlockSpec(memory_space=pltpu.VMEM)
     smem = pl.BlockSpec(memory_space=pltpu.SMEM)
     *video, key_grad, value_grad = pl.pallas_call(

time: 125 us -> 130 us (1.040)
  the two profiles are of different devices: /device:TPU:1 before, /device:TPU:6 now
where the time goes in v3:
time: 130 us
  Pallas kernels  117 us (90%)
  local copies, waits for them, and re-layouts  12.2 us (9%)
    pallas_call x1, Pallas kernels, local(): pl.pallas_call(functools.partial(kernel, sizes), out_shape=(jax.ShapeDtyp...  117 us
    unnamed x25, local copies, waits for them, and re-layouts  12.1 us

profile of v3, /device:TPU:6, one launch (start us, length us, event | category | flops | bytes accessed | tf_op | source)
XLA Modules:
  0.0 129.9 jit_solution(3229031585744970225)
XLA Ops:
  0.6 0.0 copy-start.3
  0.6 0.0 copy-start.1
  0.7 0.0 copy-start.2
  0.7 1.1 copy_dynamic-update-slice_fusion.5
  1.7 1.0 copy_dynamic-update-slice_fusion.4
  2.7 1.0 copy_dynamic-update-slice_fusion.3
  3.8 0.0 copy-done.1
  3.8 0.1 copy_dynamic-update-slice_fusion.2
  3.8 0.0 copy-done.2
  3.8 0.1 copy_dynamic-update-slice_fusion.1
  3.9 0.0 copy-done.3
  3.9 0.1 copy_dynamic-update-slice_fusion
  4.0 0.0 copy-start
  4.0 1.1 copy-done
  5.1 117.0 %shard_map.163 = (bf16[8,128,128]{2,1,0:T(8,128)(2,1)}, bf16[8,128,128]{2,1,0:T(8,128)(2,1)}, bf16[8,128,128]{2,1,0:T(8,128)(2,1)}, bf16[8,128,128]{2,1,0:T(8,12...) custom-call(bf16[8,6,128,128]{3,2,1,0:T(8,128)(2,1)} %bitcast.15, bf16[64,4096]{1,0:T(8,128)(2,1)} %bitcast.16, ...), custom_call_target="tpu_custom_call" | custom-call | tf_op jit(solution)/shard_map/pallas_call | solution.py:267
  122.1 0.0 copy-start.4
  122.1 0.0 copy-start.6
  122.1 0.0 copy-start.5
  122.1 1.9 %copy.24 = bf16[1,128,8,128]{3,2,1,0:T(8,128)(2,1)} copy(bf16[1,128,8,128]{3,1,2,0:T(8,128)(2,1)} %bitcast.20) | data formatting | bytes 524288
  124.0 1.8 %copy.25 = bf16[1,128,8,128]{3,2,1,0:T(8,128)(2,1)} copy(bf16[1,128,8,128]{3,1,2,0:T(8,128)(2,1)} %bitcast.19) | data formatting | bytes 524288
  125.8 1.8 %copy.26 = bf16[1,128,8,128]{3,2,1,0:T(8,128)(2,1)} copy(bf16[1,128,8,128]{3,1,2,0:T(8,128)(2,1)} %bitcast.18) | data formatting | bytes 524288
  127.7 0.0 copy-done.4
  127.7 0.9 copy.27
  128.5 0.0 copy-done.6
  128.5 0.7 copy.41
  129.2 0.0 copy-done.5
  129.2 0.7 copy.42
Async XLA Ops:
  0.6 3.3 %copy-start.3 = (bf16[1,128,8,128]{3,2,1,0:T(8,128)(2,1)S(1)}, bf16[1,128,8,128]{3,2,1,0:T(8,128)(2,1)}, u32[]{:S(2)}) copy-start(bf16[1,128,8,128]{3,2,1,0:T(8,128)(2,1)} %param.17) | copy-start | bytes 786436
  0.6 3.1 %copy-start.1 = (bf16[1,128,8,128]{3,2,1,0:T(8,128)(2,1)S(1)}, bf16[1,128,8,128]{3,2,1,0:T(8,128)(2,1)}, u32[]{:S(2)}) copy-start(bf16[1,128,8,128]{3,2,1,0:T(8,128)(2,1)} %param.16) | copy-start | bytes 786436
  0.7 3.2 %copy-start.2 = (bf16[1,128,8,128]{3,2,1,0:T(8,128)(2,1)S(1)}, bf16[1,128,8,128]{3,2,1,0:T(8,128)(2,1)}, u32[]{:S(2)}) copy-start(bf16[1,128,8,128]{3,2,1,0:T(8,128)(2,1)} %param.15) | copy-start | bytes 786436
  4.0 1.1 copy-start
  122.1 5.6 %copy-start.4 = (bf16[8,128,128]{2,1,0:T(8,128)(2,1)S(1)}, bf16[8,128,128]{2,1,0:T(8,128)(2,1)}, u32[]{:S(2)}) copy-start(bf16[8,128,128]{2,1,0:T(8,128)(2,1)} %get-tuple-element.15) | copy-start | bytes 786436
  122.1 6.4 %copy-start.6 = (f32[256,128]{1,0:T(8,128)S(1)}, f32[256,128]{1,0:T(8,128)}, u32[]{:S(2)}) copy-start(f32[256,128]{1,0:T(8,128)} %get-tuple-element.34) | copy-start | bytes 393220
  122.1 7.1 %copy-start.5 = (f32[256,128]{1,0:T(8,128)S(1)}, f32[256,128]{1,0:T(8,128)}, u32[]{:S(2)}) copy-start(f32[256,128]{1,0:T(8,128)} %get-tuple-element.35) | copy-start | bytes 393220

commit v4 on v2

--- a/solution.py
+++ b/solution.py
@@ -93,13 +93,13 @@
     self_y, cross_y = {}, {}
     for k in ys:
         to = lax.rem(q + k, ny)
-        cross_y[k] = push(
-            blocks.at[to, pl.ds(4, 2)], inbuf.at[pl.ds(4, 2), rows(q, part)], at_y(k)
+        self_y[k] = push(
+            blocks.at[to, pl.ds(0, 4)], inbuf.at[pl.ds(0, 4), rows(q, part)], at_y(k)
         )
     for k in ys:
         to = lax.rem(q + k, ny)
-        self_y[k] = push(
-            blocks.at[to, pl.ds(0, 4)], inbuf.at[pl.ds(0, 4), rows(q, part)], at_y(k)
+        cross_y[k] = push(
+            blocks.at[to, pl.ds(4, 2)], inbuf.at[pl.ds(4, 2), rows(q, part)], at_y(k)
         )
     own[0].wait()
     own[1].wait()
@@ -128,29 +128,6 @@
     own[2].wait()
     own[3].wait()
 
-    def normalize(i):
-        values = capbuf[i].astype(f32)
-        mean = jnp.mean(values * values, axis=-1, keepdims=True)
-        normed[rows(i, cap_rows), :] = (
-            values * lax.rsqrt(mean + norm_epsilon) * gain[...]
-        ).astype(bf16)
-
-    normalize(q)
-    for k in reversed(ys):
-        for copy in passed[k]:
-            copy.wait_recv()
-        normalize(lax.rem(q + ny - k, ny))
-    for copy in w_pair:
-        copy.wait_recv()
-    text_block = math.gcd(captions, 256)
-
-    def project(i, carry):
-        span = rows(i, text_block)
-        text[span, :] = dot(normed[span, :], wbuf[...], (1, 0)).astype(bf16)
-        return carry
-
-    lax.fori_loop(0, captions // text_block, project, 0)
-
     def attend(key, value, query_ref, cot_ref, limit, keys, query_out):
         block = math.gcd(tokens, 256)
         key_turned[:, :keys] = key[...].astype(f32).T.astype(bf16)
@@ -189,6 +166,38 @@
         kept.append(copy)
 
     for k in ys:
+        self_y[k].wait_recv()
+    attend(inbuf.at[1], inbuf.at[2], inbuf.at[0], inbuf.at[3], video_limit, tokens, grads.at[0])
+    give(0, query_out)
+    grads[1] = key_total[...].astype(bf16)
+    give(1, key_out)
+    grads[2] = value_total[...].astype(bf16)
+    give(2, value_out)
+
+    def normalize(i):
+        values = capbuf[i].astype(f32)
+        mean = jnp.mean(values * values, axis=-1, keepdims=True)
+        normed[rows(i, cap_rows), :] = (
+            values * lax.rsqrt(mean + norm_epsilon) * gain[...]
+        ).astype(bf16)
+
+    normalize(q)
+    for k in reversed(ys):
+        for copy in passed[k]:
+            copy.wait_recv()
+        normalize(lax.rem(q + ny - k, ny))
+    for copy in w_pair:
+        copy.wait_recv()
+    text_block = math.gcd(captions, 256)
+
+    def project(i, carry):
+        span = rows(i, text_block)
+        text[span, :] = dot(normed[span, :], wbuf[...], (1, 0)).astype(bf16)
+        return carry
+
+    lax.fori_loop(0, captions // text_block, project, 0)
+
+    for k in ys:
         cross_y[k].wait_recv()
     attend(
         text.at[:, pl.ds(0, size)], text.at[:, pl.ds(size, size)], inbuf.at[4], inbuf.at[5],
@@ -219,14 +228,6 @@
         if i:
             finish(i - 1)
     finish(nz - 1)
-    for k in ys:
-        self_y[k].wait_recv()
-    attend(inbuf.at[1], inbuf.at[2], inbuf.at[0], inbuf.at[3], video_limit, tokens, grads.at[0])
-    give(0, query_out)
-    grads[1] = key_total[...].astype(bf16)
-    give(1, key_out)
-    grads[2] = value_total[...].astype(bf16)
-    give(2, value_out)
     total = mine[nz - 1]
     for i, copy in enumerate(ring):
         copy.wait_recv()

time: 125 us -> 123 us (0.984)
  Pallas kernels: 112 us -> 110 us
    pallas_call x1, Pallas kernels: 112 us -> 110 us  [local(): pl.pallas_call(functools.partial(kernel, sizes), out_shape=(jax.ShapeDtyp...]
where the time goes in v4:
time: 123 us
  Pallas kernels  110 us (89%)
  local copies, waits for them, and re-layouts  12.2 us (10%)
    pallas_call x1, Pallas kernels, local(): pl.pallas_call(functools.partial(kernel, sizes), out_shape=(jax.ShapeDtyp...  110 us
    unnamed x25, local copies, waits for them, and re-layouts  12.1 us

profile of v4, /device:TPU:1, one launch (start us, length us, event | category | flops | bytes accessed | tf_op | source)
XLA Modules:
  0.0 122.7 jit_solution(10819519830458549616)
XLA Ops:
  0.6 0.0 copy-start.3
  0.6 0.0 copy-start.1
  0.7 0.0 copy-start.2
  0.7 1.1 copy_dynamic-update-slice_fusion.5
  1.7 1.0 copy_dynamic-update-slice_fusion.4
  2.7 1.0 copy_dynamic-update-slice_fusion.3
  3.8 0.0 copy-done.1
  3.8 0.1 copy_dynamic-update-slice_fusion.2
  3.8 0.0 copy-done.2
  3.8 0.1 copy_dynamic-update-slice_fusion.1
  3.9 0.0 copy-done.3
  3.9 0.1 copy_dynamic-update-slice_fusion
  4.0 0.0 copy-start
  4.0 1.1 copy-done
  5.1 109.8 %shard_map.163 = (bf16[8,128,128]{2,1,0:T(8,128)(2,1)}, bf16[8,128,128]{2,1,0:T(8,128)(2,1)}, bf16[8,128,128]{2,1,0:T(8,128)(2,1)}, bf16[8,128,128]{2,1,0:T(8,12...) custom-call(bf16[8,6,128,128]{3,2,1,0:T(8,128)(2,1)} %bitcast.15, bf16[64,4096]{1,0:T(8,128)(2,1)} %bitcast.16, ...), custom_call_target="tpu_custom_call" | custom-call | tf_op jit(solution)/shard_map/pallas_call | solution.py:263
  114.9 0.0 copy-start.4
  114.9 0.0 copy-start.6
  114.9 0.0 copy-start.5
  114.9 1.9 %copy.24 = bf16[1,128,8,128]{3,2,1,0:T(8,128)(2,1)} copy(bf16[1,128,8,128]{3,1,2,0:T(8,128)(2,1)} %bitcast.20) | data formatting | bytes 524288
  116.8 1.8 %copy.25 = bf16[1,128,8,128]{3,2,1,0:T(8,128)(2,1)} copy(bf16[1,128,8,128]{3,1,2,0:T(8,128)(2,1)} %bitcast.19) | data formatting | bytes 524288
  118.6 1.8 %copy.26 = bf16[1,128,8,128]{3,2,1,0:T(8,128)(2,1)} copy(bf16[1,128,8,128]{3,1,2,0:T(8,128)(2,1)} %bitcast.18) | data formatting | bytes 524288
  120.5 0.0 copy-done.4
  120.5 0.9 copy.27
  121.3 0.0 copy-done.6
  121.4 0.7 copy.41
  122.0 0.0 copy-done.5
  122.0 0.7 copy.42
Async XLA Ops:
  0.6 3.3 %copy-start.3 = (bf16[1,128,8,128]{3,2,1,0:T(8,128)(2,1)S(1)}, bf16[1,128,8,128]{3,2,1,0:T(8,128)(2,1)}, u32[]{:S(2)}) copy-start(bf16[1,128,8,128]{3,2,1,0:T(8,128)(2,1)} %param.17) | copy-start | bytes 786436
  0.6 3.1 %copy-start.1 = (bf16[1,128,8,128]{3,2,1,0:T(8,128)(2,1)S(1)}, bf16[1,128,8,128]{3,2,1,0:T(8,128)(2,1)}, u32[]{:S(2)}) copy-start(bf16[1,128,8,128]{3,2,1,0:T(8,128)(2,1)} %param.16) | copy-start | bytes 786436
  0.7 3.2 %copy-start.2 = (bf16[1,128,8,128]{3,2,1,0:T(8,128)(2,1)S(1)}, bf16[1,128,8,128]{3,2,1,0:T(8,128)(2,1)}, u32[]{:S(2)}) copy-start(bf16[1,128,8,128]{3,2,1,0:T(8,128)(2,1)} %param.15) | copy-start | bytes 786436
  4.0 1.1 copy-start
  114.9 5.6 %copy-start.4 = (bf16[8,128,128]{2,1,0:T(8,128)(2,1)S(1)}, bf16[8,128,128]{2,1,0:T(8,128)(2,1)}, u32[]{:S(2)}) copy-start(bf16[8,128,128]{2,1,0:T(8,128)(2,1)} %get-tuple-element.15) | copy-start | bytes 786436
  114.9 6.4 %copy-start.6 = (f32[256,128]{1,0:T(8,128)S(1)}, f32[256,128]{1,0:T(8,128)}, u32[]{:S(2)}) copy-start(f32[256,128]{1,0:T(8,128)} %get-tuple-element.34) | copy-start | bytes 393220
  114.9 7.1 %copy-start.5 = (f32[256,128]{1,0:T(8,128)S(1)}, f32[256,128]{1,0:T(8,128)}, u32[]{:S(2)}) copy-start(f32[256,128]{1,0:T(8,128)} %get-tuple-element.35) | copy-start | bytes 393220
